TPU v7x, 256 devices: a whole 4x4x8 slice. The times are simulated.
256 devices in a mesh: seq: 16 (over y, x), fsdp: 16 (over z, core).
Axes of the slice: x: 4, y: 4, z: 8, core: 2. Of those that a mesh axis runs over, the one named last changes fastest.
Arguments:
- kv_cache: bfloat16 [2, 32, 8192, 1280], P(None, 'fsdp', 'seq'), may hold values from -6 to 6
- keep_flags: int32 [32, 8192], P('fsdp', 'seq'), may hold values from 0 to 1, as said below
- block_weights: float32 [32, 8192], P('fsdp', 'seq'), may hold values from 0.05 to 2
- lengths: int32 [32], P('fsdp'), may hold values from 2048 to 8192, as said below
- token_qkv: bfloat16 [32, 3840], P('fsdp'), may hold values from -10 to 10
- stream: bfloat16 [32, 1280], P('fsdp'), may hold values from -0.59765625 to 0.59765625
- w_out: bfloat16 [1280, 1280], P(None, 'fsdp'), may hold values from -0.15625 to 0.15625
- w_up: bfloat16 [1280, 1280], P(None, 'fsdp'), may hold values from -0.15625 to 0.15625
- w_down: bfloat16 [1280, 1280], P(None, 'fsdp'), may hold values from -0.15625 to 0.15625
- w_qkv: bfloat16 [1280, 3840], P(None, 'fsdp'), may hold values from -0.15625 to 0.15625
- mlp_gain: float32 [1280], replicated, may hold values from 0.1 to 1.9
- next_gain: float32 [1280], replicated, may hold values from 0.1 to 1.9
Outputs:
- packed_cache: bfloat16 [2, 32, 8192, 1280], P(None, 'fsdp', 'seq')
- block_summary: bfloat16 [2, 32, 512, 1280], P(None, 'fsdp', 'seq')
- layer_out: bfloat16 [32, 1280], P('fsdp', 'seq')
- next_qkv: bfloat16 [32, 3840], P('fsdp', 'seq')
Inputs may be any that keep to these rules, and one draw needn't show every extreme that they name: `keep_flags`: in every draw one request keeps all 512 positions of one aligned block of 512 positions. `lengths`: in every draw some request has 8192 filled positions.
All inputs are finite; a program needn't handle non-finite values.
Results may differ from a plain program's by a relative error of at most 0.02.
Values may be sent and summed in bfloat16 or wider, within the bound.
A program may use at most 128 MiB of HBM per device.

v0:
```python
import math
import jax
import jax.numpy as jnp
from jax import lax
from jax.sharding import PartitionSpec as P

H = 16
BLK = 16
neg_fill = -1e30


def combined_all(part, axis, combine):
    gathered = jax.tree.map(lambda a: lax.all_gather(a, axis), part)

    def take(source):
        return jax.tree.map(lambda a: lax.dynamic_index_in_dim(a, source, 0, False), gathered)

    return lax.fori_loop(
        1, lax.axis_size(axis), lambda source, state: combine(state, take(source)), take(0)
    )


def normalize(values, gain):
    wide = values.astype(jnp.float32)
    factor = lax.rsqrt(jnp.mean(wide * wide, axis=-1, keepdims=True) + 1e-06)
    return (wide * factor * gain).astype(jnp.bfloat16)


def combine_parts(first, second):
    peak_a, total_a, accum_a = first
    peak_b, total_b, accum_b = second
    peak = jnp.maximum(peak_a, peak_b)
    factor_a = jnp.exp(peak_a - peak)
    factor_b = jnp.exp(peak_b - peak)
    return (
        peak,
        total_a * factor_a + total_b * factor_b,
        accum_a * factor_a[..., None] + accum_b * factor_b[..., None],
    )


def partial_softmax(queries, keys, values, usable, inv_root):
    scores = (
        jnp.einsum("rhe,rnhe->rhn", queries, keys, preferred_element_type=jnp.float32) * inv_root
    )
    scores = jnp.where(usable[:, None, :], scores, neg_fill)
    peak = jnp.max(scores, axis=-1)
    expo = jnp.where(usable[:, None, :], jnp.exp(scores - peak[..., None]), 0.0)
    total = jnp.sum(expo, axis=-1)
    accum = jnp.einsum("rhn,rnhe->rhe", expo, values, preferred_element_type=jnp.float32)
    return (peak, total, accum)


def split_heads(block):
    return block.reshape(block.shape[:-1] + (H, block.shape[-1] // H))


def body(
    kv_cache,
    keep_flags,
    block_weights,
    lengths,
    token_qkv,
    stream,
    w_out,
    w_up,
    w_down,
    w_qkv,
    mlp_gain,
    next_gain,
):
    seq_count = lax.axis_size("seq")
    seq_here = lax.axis_index("seq")
    reqs = kv_cache.shape[1]
    rows = kv_cache.shape[2]
    width = kv_cache.shape[3]
    head_size = width // H
    inv_root = 1.0 / math.sqrt(head_size)
    position = seq_here * rows + jnp.arange(rows, dtype=jnp.int32)
    in_range = position[None, :] < lengths[:, None]
    kept_rows = in_range & (keep_flags == 1)
    drop_rows = in_range & (keep_flags == 0)
    inclusive = jnp.cumsum(kept_rows.astype(jnp.int32), axis=1)
    held = inclusive[:, -1]
    every = lax.all_gather(held[None, :], "seq", axis=0, tiled=True)
    lower = jnp.arange(seq_count, dtype=jnp.int32)[:, None] < seq_here
    before = jnp.sum(jnp.where(lower, every, 0), axis=0)
    blocks = rows // BLK
    drop_weight = jnp.where(drop_rows, block_weights, 0.0).reshape(reqs, blocks, BLK)
    weight_total = jnp.sum(drop_weight, axis=-1)
    drop_count = jnp.sum(drop_rows.reshape(reqs, blocks, BLK).astype(jnp.int32), axis=-1)
    sums = jnp.einsum(
        "rbk,crbkd->crbd",
        drop_weight,
        kv_cache.reshape(2, reqs, blocks, BLK, width),
        preferred_element_type=jnp.float32,
        precision=lax.Precision.HIGHEST,
    )
    block_summary = (sums / jnp.maximum(weight_total, 1.0)[None, :, :, None]).astype(jnp.bfloat16)
    queries = split_heads(token_qkv[:, :width])
    own_keys = split_heads(token_qkv[:, width : 2 * width])
    own_values = split_heads(token_qkv[:, 2 * width :])
    slot = rows // seq_count
    target = jnp.arange(seq_count, dtype=jnp.int32)
    offset = jnp.mod(target[:, None] - before[None, :], seq_count)
    sent = (held[None, :] - offset + seq_count - 1) // seq_count
    wanted = offset[:, :, None] + seq_count * jnp.arange(slot, dtype=jnp.int32)[None, None, :]
    local_rank = inclusive - 1
    wanted_r = jnp.transpose(wanted, (1, 0, 2))
    pick_send = (
        kept_rows[:, None, None, :] & (local_rank[:, None, None, :] == wanted_r[:, :, :, None])
    ).astype(jnp.bfloat16)
    outgoing = jnp.einsum(
        "rtsp,crpd->ctrsd", pick_send, kv_cache, preferred_element_type=jnp.float32
    ).astype(jnp.bfloat16)
    incoming, arrived = (
        lax.all_to_all(outgoing, "seq", split_axis=1, concat_axis=1, tiled=True),
        lax.all_to_all(sent[None], "seq", split_axis=1, concat_axis=1, tiled=True),
    )
    counts_in = arrived[0]
    ends = jnp.cumsum(counts_in, axis=0)
    starts = ends - counts_in
    filled = ends[-1]
    local_rows = jnp.arange(rows, dtype=jnp.int32)
    slot_index = jnp.arange(slot, dtype=jnp.int32)
    starts_r = starts.T
    counts_r = counts_in.T
    valid_slot = slot_index[None, None, :] < counts_r[:, :, None]
    dest_row = starts_r[:, :, None] + slot_index[None, None, :]
    pick_recv = (
        valid_slot[:, None, :, :] & (dest_row[:, None, :, :] == local_rows[None, :, None, None])
    ).astype(jnp.bfloat16)
    packed_cache = jnp.einsum(
        "rlts,ctrsd->crld", pick_recv, incoming, preferred_element_type=jnp.float32
    ).astype(jnp.bfloat16)
    present = local_rows[None, :] < filled[:, None]
    row_part = partial_softmax(
        queries, split_heads(packed_cache[0]), split_heads(packed_cache[1]), present, inv_root
    )
    summary_part = partial_softmax(
        queries,
        split_heads(block_summary[0]),
        split_heads(block_summary[1]),
        drop_count > 0,
        inv_root,
    )
    peak, total, accum = combined_all(combine_parts(row_part, summary_part), "seq", combine_parts)
    own_score = (
        jnp.einsum("rhe,rhe->rh", queries, own_keys, preferred_element_type=jnp.float32) * inv_root
    )
    top_score = jnp.maximum(peak, own_score)
    factor_old = jnp.exp(peak - top_score)
    factor_own = jnp.exp(own_score - top_score)
    attended = (
        accum * factor_old[..., None] + factor_own[..., None] * own_values.astype(jnp.float32)
    ) / (total * factor_old + factor_own)[..., None]
    attended = attended.reshape(reqs, width).astype(jnp.bfloat16)
    fsdp_here = lax.axis_index("fsdp")

    def widen(columns):
        return lax.all_gather(columns, "fsdp", axis=1, tiled=True)

    def own_columns(full, count):
        return lax.dynamic_slice_in_dim(full, fsdp_here * count, count, 1)

    attn_all, stream_all = (
        lax.all_gather(attended, "fsdp", axis=0, tiled=True),
        lax.all_gather(stream, "fsdp", axis=0, tiled=True),
    )
    mid_cols = own_columns(stream_all, w_out.shape[1]).astype(jnp.float32) + jnp.dot(
        attn_all, w_out, preferred_element_type=jnp.float32
    )
    mid = widen(mid_cols.astype(jnp.bfloat16))
    hidden = widen(
        jax.nn.silu(
            jnp.dot(normalize(mid, mlp_gain), w_up, preferred_element_type=jnp.float32)
        ).astype(jnp.bfloat16)
    )
    out_cols = own_columns(mid, w_down.shape[1]).astype(jnp.float32) + jnp.dot(
        hidden, w_down, preferred_element_type=jnp.float32
    )
    layer_all = widen(out_cols.astype(jnp.bfloat16))
    qkv_all = widen(
        jnp.dot(normalize(layer_all, next_gain), w_qkv, preferred_element_type=jnp.float32).astype(
            jnp.bfloat16
        )
    )
    layer_rows = lax.dynamic_slice_in_dim(layer_all, fsdp_here * reqs, reqs, 0)
    qkv_rows = lax.dynamic_slice_in_dim(qkv_all, fsdp_here * reqs, reqs, 0)
    layer_width = width // seq_count
    qkv_width = 3 * width // seq_count
    layer_out = lax.dynamic_slice_in_dim(layer_rows, seq_here * layer_width, layer_width, 1)
    next_qkv = lax.dynamic_slice_in_dim(qkv_rows, seq_here * qkv_width, qkv_width, 1)
    return (packed_cache, block_summary, layer_out, next_qkv)


def solution(mesh):
    placed = (
        P(None, "fsdp", "seq", None),
        P("fsdp", "seq"),
        P("fsdp", "seq"),
        P("fsdp"),
        P("fsdp", None),
        P("fsdp", None),
        P(None, "fsdp"),
        P(None, "fsdp"),
        P(None, "fsdp"),
        P(None, "fsdp"),
        P(),
        P(),
    )
    return jax.shard_map(
        body,
        mesh=mesh,
        in_specs=placed,
        out_specs=(
            P(None, "fsdp", "seq", None),
            P(None, "fsdp", "seq", None),
            P("fsdp", "seq"),
            P("fsdp", "seq"),
        ),
        check_vma=False,
    )
```

profile of v0, /device:TPU:1, one launch (start us, length us, event | category | flops | bytes accessed | tf_op | source)
XLA Modules:
  0.0 290.0 jit_solution(1825323752103344393)
XLA Ops:
  0.7 0.8 fusion.76
  1.5 0.6 reduce-window.6
  2.1 0.2 slice_reduce_fusion
  2.4 0.2 reduce-window.9
  2.7 0.1 copy.79
  2.8 1.3 dynamic-slice
  4.7 0.1 bitcast_dynamic-update-slice_fusion
  4.8 13.9 %all-reduce = s32[32]{0:T(128)S(1)} all-reduce(s32[32]{0:T(128)S(1)} %bitcast_dynamic-update-slice_fusion), channel_id=2, replica_groups=mesh['seq'=16,'fsdp'=16] {'seq'}, use_global_device_ids=true, to_apply=%add | all-reduce | flops 32 | bytes 256
  18.8 0.1 select_reduce_fusion
  18.9 0.7 and_select_fusion
  19.6 3.5 %all-to-all-start.1 = ((s32[1,16,2]{2,0,1:T(1,128)}), s32[1,16,2]{2,0,1:T(1,128)S(1)}, u32[]{:S(2)}, u32[]{:S(2)}) async-start(s32[1,16,2]{2,0,1:T(1,128)} %and_select_fusion), calls=%async_computation.1 | async-start | bytes 16384 | tf_op jit(solution)/shard_map/all_to_all | solution.py:118
  23.2 5.4 %fusion.7 = bf16[2,16,2,32,1280]{4,3,1,0,2:T(8,128)(2,1)S(1)} fusion(s32[2,16,32]{2,1,0:T(8,128)S(1)} %broadcast_add_fusion, s32[2,512]{1,0:T(2,128)S(1)} %broadcast_add_fusion.1, pred[2,512]{1,0:T(4,128)(4,1)S(1)} %get-tuple-element.236, bf16[2,2,512,1280]{3,2,1,0:T(8,128)(2,1)} %param.14), kind=kOutput, calls=%fused_computation.15 | convolution fusion | flops 2688024576 | bytes 10494976 | tf_op jit(solution)/shard_map/rtsp,crpd->ctrsd/dot_general | solution.py:113
  28.6 2.8 copy.45
  31.5 6.8 %all-to-all-start = ((bf16[2,16,2,32,1280]{4,3,0,2,1:T(8,128)(2,1)}), bf16[2,16,2,32,1280]{4,3,0,2,1:T(8,128)(2,1)}, u32[]{:S(2)}, u32[]{:S(2)}) async-start(bf16[2,16,2,32,1280]{4,3,0,2,1:T(8,128)(2,1)} %copy.45), calls=%async_computation | async-start | bytes 10485760 | tf_op jit(solution)/shard_map/all_to_all | solution.py:117
  38.5 0.1 reshape.406
  38.8 4.8 %fusion.5 = f32[2,32,1,2,1280]{4,2,3,1,0:T(1,128)S(1)} fusion(f32[2,32,16,1,1]{2,3,4,1,0:T(1,128)S(1)} %bitcast.193, bf16[2,2,32,16,1280]{4,3,2,1,0:T(8,128)(2,1)} %bitcast.190), kind=kOutput, calls=%fused_computation.13 | convolution fusion | flops 31457280 | bytes 5902336 | tf_op jit(solution)/shard_map/rbk,crbkd->crbd/dot_general | solution.py:92
  43.6 0.1 fusion.28
  43.7 0.7 copy-done.2
  44.4 0.4 reshape_squeeze.13
  44.9 0.1 reduce_sum.69
  45.0 0.4 reshape_squeeze.15
  45.6 24.9 %all-gather.2 = bf16[16,2,1280]{2,1,0:T(2,128)(2,1)S(1)} all-gather(bf16[1,2,1280]{2,1,0:T(2,128)(2,1)S(1)} %bitcast.202), channel_id=1, replica_groups=mesh['seq'=16,'fsdp'=16] {'fsdp'}, dimensions={0}, use_global_device_ids=true | all-gather | bytes 87040 | tf_op jit(solution)/shard_map/all_gather | solution.py:168
  70.6 0.7 fusion.54
  71.2 0.2 fusion.31
  71.5 0.1 fusion.60
  71.6 0.8 fusion.75
  72.3 0.8 fusion.29
  73.7 30.8 %all-to-all-done = bf16[2,16,2,32,1280]{4,3,0,2,1:T(8,128)(2,1)} async-done(((bf16[2,16,2,32,1280]{4,3,0,2,1:T(8,128)(2,1)}), bf16[2,16,2,32,1280]{4,3,0,2,1:T(8,128)(2,1)}, u32[]{:S(2)}, u32[]{:S(2)}) %all-to-all-start) | async-done | bytes 5242912 | tf_op jit(solution)/shard_map/all_to_all | solution.py:117
  104.5 5.7 %fusion.12 = bf16[2,2,1280,512,1]{3,2,1,0,4:T(8,128)(2,1)S(1)} fusion(bf16[2,16,2,32,1280]{4,3,0,2,1:T(8,128)(2,1)} %all-to-all-done, s32[2,16,32]{2,0,1:T(2,128)S(1)} %iota_add_fusion, pred[2,16,32]{2,0,1:T(4,128)(4,1)S(1)} %iota_compare_fusion.1), kind=kOutput, calls=%fused_computation.19 | convolution fusion | flops 2685403136 | bytes 10490880 | tf_op jit(solution)/shard_map/rlts,ctrsd->crld/dot_general | solution.py:133
  110.2 0.3 copy.109
  110.5 0.3 fusion.78
  110.9 1.9 copy-done.1
  112.8 0.4 fusion.81
  113.3 0.1 fusion.53
  113.4 0.7 fusion.51
  114.1 0.6 fusion.64
  114.7 0.7 fusion.52
  115.4 7.9 %copy.55 = bf16[2,2,512,1280]{3,2,1,0:T(8,128)(2,1)} copy(bf16[2,2,512,1280]{2,3,1,0:T(8,128)(2,1)} %bitcast.188) | data formatting | bytes 10485760
  123.3 1.5 fusion.49
  124.9 0.8 multiply_add_fusion
  125.7 18.9 %all-gather.1 = f32[32,16,80]{2,1,0:T(8,128)S(1)} all-gather(f32[2,16,80]{2,1,0:T(8,128)S(1)} %multiply_add_fusion), channel_id=3, replica_groups=mesh['seq'=16,'fsdp'=16] {'seq'}, dimensions={0}, use_global_device_ids=true | all-gather | bytes 174080 | tf_op jit(solution)/shard_map/all_gather | solution.py:13
  144.6 0.7 fusion.69
  145.3 16.3 %all_gather.38 = f32[16,2,16]{2,1,0:T(2,128)S(1)} all-gather(f32[1,2,16]{2,1,0:T(2,128)S(1)} %get-tuple-element.239), channel_id=1, replica_groups=mesh['seq'=16,'fsdp'=16] {'seq'}, dimensions={0}, use_global_device_ids=true | all-gather | bytes 2176 | tf_op jit(solution)/shard_map/all_gather | solution.py:13
  161.6 16.5 %all_gather.37 = f32[16,2,16]{2,1,0:T(2,128)S(1)} all-gather(f32[1,2,16]{2,1,0:T(2,128)S(1)} %get-tuple-element.240), channel_id=1, replica_groups=mesh['seq'=16,'fsdp'=16] {'seq'}, dimensions={0}, use_global_device_ids=true | all-gather | bytes 2176 | tf_op jit(solution)/shard_map/all_gather | solution.py:13
  178.1 1.5 while.19
  179.6 0.7 multiply_add_fusion.1
  180.5 41.5 %all-gather.3 = bf16[16,2,1280]{2,1,0:T(2,128)(2,1)S(1)} all-gather(bf16[1,2,1280]{2,1,0:T(2,128)(2,1)S(1)} %reshape.375), channel_id=1, replica_groups=mesh['seq'=16,'fsdp'=16] {'fsdp'}, dimensions={0}, use_global_device_ids=true | all-gather | bytes 87040 | tf_op jit(solution)/shard_map/all_gather | solution.py:167
  222.1 0.2 fusion.21
  222.3 14.8 %all-gather.4 = bf16[16,80,32]{1,2,0:T(8,128)(2,1)S(1)} all-gather(bf16[1,80,32]{1,2,0:T(8,128)(2,1)S(1)} %fusion.21), channel_id=1, replica_groups=mesh['seq'=16,'fsdp'=16] {'fsdp'}, dimensions={0}, use_global_device_ids=true | all-gather | bytes 87040 | tf_op jit(solution)/shard_map/all_gather | solution.py:161
  237.1 0.2 reshape.378
  237.3 0.1 fusion.33
  237.4 1.2 fusion.57
  238.7 16.1 %all-gather.5 = bf16[16,80,32]{1,2,0:T(8,128)(2,1)S(1)} all-gather(bf16[1,80,32]{1,2,0:T(8,128)(2,1)S(1)} %fusion.57), channel_id=1, replica_groups=mesh['seq'=16,'fsdp'=16] {'fsdp'}, dimensions={0}, use_global_device_ids=true | all-gather | bytes 87040 | tf_op jit(solution)/shard_map/all_gather | solution.py:161
  254.9 0.2 reshape.380
  255.0 1.1 fusion.20
  256.2 14.8 %all-gather.6 = bf16[16,80,32]{1,2,0:T(8,128)(2,1)S(1)} all-gather(bf16[1,80,32]{1,2,0:T(8,128)(2,1)S(1)} %fusion.20), channel_id=1, replica_groups=mesh['seq'=16,'fsdp'=16] {'fsdp'}, dimensions={0}, use_global_device_ids=true | all-gather | bytes 87040 | tf_op jit(solution)/shard_map/all_gather | solution.py:161
  271.0 0.2 reshape.382
  271.2 0.1 fusion.37
  271.4 0.3 fusion.17
  271.6 16.6 %all-gather.7 = bf16[16,240,32]{1,2,0:T(8,128)(2,1)S(1)} all-gather(bf16[1,240,32]{1,2,0:T(8,128)(2,1)S(1)} %fusion.17), channel_id=1, replica_groups=mesh['seq'=16,'fsdp'=16] {'fsdp'}, dimensions={0}, use_global_device_ids=true | all-gather | bytes 261120 | tf_op jit(solution)/shard_map/all_gather | solution.py:161
  288.2 0.1 copy.54
  288.4 0.4 reshape.384
  288.7 0.6 dynamic-slice_bitcast_fusion.1
  289.3 0.6 dynamic-slice_bitcast_fusion
  (96 shorter events, 3.5 us)
Async XLA Ops:
  0.6 270.7 %copy-start = (bf16[1280,240]{0,1:T(8,128)(2,1)S(1)}, bf16[1280,240]{0,1:T(8,128)(2,1)}, u32[]{:S(2)}) copy-start(bf16[1280,240]{0,1:T(8,128)(2,1)} %param.23) | copy-start | bytes 1843204
  19.6 11.9 %all-to-all-start.1 = ((s32[1,16,2]{2,0,1:T(1,128)}), s32[1,16,2]{2,0,1:T(1,128)S(1)}, u32[]{:S(2)}, u32[]{:S(2)}) async-start(s32[1,16,2]{2,0,1:T(1,128)} %and_select_fusion), calls=%async_computation.1 | async-start | bytes 16384 | tf_op jit(solution)/shard_map/all_to_all | solution.py:118
  31.5 6.8 %copy-start.10 = (f32[2,512]{1,0:T(2,128)S(1)}, f32[2,512]{1,0:T(2,128)}, u32[]{:S(2)}) copy-start(f32[2,512]{1,0:T(2,128)} %param.16) | copy-start | bytes 12292
  31.5 7.0 %copy-start.7 = (bf16[2,3840]{1,0:T(2,128)(2,1)S(1)}, bf16[2,3840]{1,0:T(2,128)(2,1)}, u32[]{:S(2)}) copy-start(bf16[2,3840]{1,0:T(2,128)(2,1)} %param.18) | copy-start | bytes 46084
  31.5 73.0 %all-to-all-start = ((bf16[2,16,2,32,1280]{4,3,0,2,1:T(8,128)(2,1)}), bf16[2,16,2,32,1280]{4,3,0,2,1:T(8,128)(2,1)}, u32[]{:S(2)}, u32[]{:S(2)}) async-start(bf16[2,16,2,32,1280]{4,3,0,2,1:T(8,128)(2,1)} %copy.45), calls=%async_computation | async-start | bytes 10485760 | tf_op jit(solution)/shard_map/all_to_all | solution.py:117
  38.3 7.3 %copy-start.9 = (bf16[2,1280]{1,0:T(2,128)(2,1)S(1)}, bf16[2,1280]{1,0:T(2,128)(2,1)}, u32[]{:S(2)}) copy-start(bf16[2,1280]{1,0:T(2,128)(2,1)} %param.19) | copy-start | bytes 15364
  43.7 0.7 copy-start.2
  71.6 38.6 %copy-start.4 = (f32[2,16]{1,0:T(2,128)}, f32[2,16]{1,0:T(2,128)S(1)}, u32[]{:S(2)}) copy-start(f32[2,16]{1,0:T(2,128)S(1)} %fusion.60) | copy-start | bytes 388
  110.5 2.3 copy-start.1
  110.5 3.5 %copy-start.5 = (f32[2,16]{1,0:T(2,128)S(1)}, f32[2,16]{1,0:T(2,128)}, u32[]{:S(2)}) copy-start(f32[2,16]{1,0:T(2,128)} %copy-done.4) | copy-start | bytes 388
  115.4 29.2 %copy-start.6 = (f32[2,16]{1,0:T(2,128)S(1)}, f32[2,16]{1,0:T(2,128)}, u32[]{:S(2)}) copy-start(f32[2,16]{1,0:T(2,128)} %copy-done.4) | copy-start | bytes 388
  115.4 106.6 %copy-start.3 = (bf16[1280,80]{0,1:T(8,128)(2,1)S(1)}, bf16[1280,80]{0,1:T(8,128)(2,1)}, u32[]{:S(2)}) copy-start(bf16[1280,80]{0,1:T(8,128)(2,1)} %param.20) | copy-start | bytes 614404
  123.3 148.0 %copy-start.8 = (f32[1280]{0:T(1024)S(1)}, f32[1280]{0:T(1024)}, u32[]{:S(2)}) copy-start(f32[1280]{0:T(1024)} %param.25) | copy-start | bytes 15364
where the time goes:
time: 291 us; the launch traced here: 290 us
  blocking collectives  194 us (67%)
  waiting for transfers between devices  30.8 us (11%)
  matrix products  21.6 us (7%)
  local copies, waits for them, and re-layouts  20.2 us (7%)
  other arithmetic  11 us (4%)
  starting transfers between devices  10.2 us (4%)
    all_gather x4, blocking collectives, widen(): return lax.all_gather(columns, 'fsdp', axis=1, tiled=True)  62.3 us
    all_gather x3, blocking collectives, combined_all(): gathered = jax.tree.map(lambda a: lax.all_gather(a, axis), part)  51.7 us
    all_gather x1, blocking collectives, body(): lax.all_gather(attended, 'fsdp', axis=0, tiled=True)  41.5 us
    all_to_all x1, waiting for transfers between devices, body(): lax.all_to_all(outgoing, 'seq', split_axis=1, concat_axis=1, tiled=True)  30.8 us
    all_gather x1, blocking collectives, body(): lax.all_gather(stream, 'fsdp', axis=0, tiled=True)  24.9 us
    unnamed x1, blocking collectives  13.9 us
    unnamed x35, local copies, waits for them, and re-layouts  13.1 us
    all_to_all x1, starting transfers between devices, body(): lax.all_to_all(outgoing, 'seq', split_axis=1, concat_axis=1, tiled=True)  6.77 us
  transfers between devices with their start and end apart: 2, of which 1 were waited for; matrix products, arithmetic and copies ran while one was open for 6% of the time, Pallas kernels for 0%

commit v1 on v0

--- a/solution.py
+++ b/solution.py
@@ -7,6 +7,19 @@
 H = 16
 BLK = 16
 neg_fill = -1e30
+
+
+def ring_gather(value, axis, dim):
+    ways = lax.axis_size(axis)
+    up = [(d, (d + 1) % ways) for d in range(ways)]
+    down = [(d, (d - 1) % ways) for d in range(ways)]
+    earlier, later = ([value], [value])
+    for _ in range(ways // 2):
+        earlier.append(lax.ppermute(earlier[-1], axis, up))
+    for _ in range((ways - 1) // 2):
+        later.append(lax.ppermute(later[-1], axis, down))
+    line = jnp.concatenate([*earlier[::-1], *later[1:]], axis=dim)
+    return jnp.roll(line, (lax.axis_index(axis) - ways // 2) * value.shape[dim], axis=dim)
 
 
 def combined_all(part, axis, combine):
@@ -165,7 +178,7 @@
 
     attn_all, stream_all = (
         lax.all_gather(attended, "fsdp", axis=0, tiled=True),
-        lax.all_gather(stream, "fsdp", axis=0, tiled=True),
+        ring_gather(stream, "fsdp", 0),
     )
     mid_cols = own_columns(stream_all, w_out.shape[1]).astype(jnp.float32) + jnp.dot(
         attn_all, w_out, preferred_element_type=jnp.float32

time: 291 us -> 287 us (0.986)
  starting transfers between devices: 10.2 us -> 35.2 us
  blocking collectives: 194 us -> 169 us
  local copies, waits for them, and re-layouts: 20.2 us -> 25.4 us
  other arithmetic: 11 us -> 5.92 us
  waiting for transfers between devices: 30.8 us -> 27.5 us
    all_gather x1 -> x0, blocking collectives: 24.9 us -> none  [body(): lax.all_gather(stream, 'fsdp', axis=0, tiled=True)]
    ppermute x0 -> x15, starting transfers between devices: none -> 24.9 us  [the longest x7 13.2 us: ring_gather(): later.append(lax.ppermute(later[-1], axis, down))]
    all_to_all x1, waiting for transfers between devices: 30.8 us -> 18.4 us  [body(): lax.all_to_all(outgoing, 'seq', split_axis=1, concat_axis=1, tiled=True)]
    ppermute x0 -> x15, waiting for transfers between devices: none -> 9.06 us  [the longest x7 5.32 us: ring_gather(): later.append(lax.ppermute(later[-1], axis, down))]
    concatenate x0 -> x1, local copies, waits for them, and re-layouts: none -> 5.15 us  [ring_gather(): jnp.roll(line, (lax.axis_index(axis) - ways // 2) * value.shape[dim], axi...]
    unnamed x35 -> x30, local copies, waits for them, and re-layouts: 13.1 us -> 13.1 us
  transfers between devices with their start and end apart: 2 -> 17, of which waited for: 1 -> 10; matrix products, arithmetic and copies ran while one was open for 6% -> 7% of each run, Pallas kernels for 0% -> 0%
where the time goes in v1:
time: 287 us; the launch traced here: 286 us
  blocking collectives  169 us (59%)
  starting transfers between devices  35.2 us (12%)
  waiting for transfers between devices  27.5 us (10%)
  local copies, waits for them, and re-layouts  25.4 us (9%)
  matrix products  21 us (7%)
  other arithmetic  5.92 us (2%)
    all_gather x4, blocking collectives, widen(): return lax.all_gather(columns, 'fsdp', axis=1, tiled=True)  62.3 us
    all_gather x3, blocking collectives, combined_all(): gathered = jax.tree.map(lambda a: lax.all_gather(a, axis), part)  51.9 us
    all_gather x1, blocking collectives, body(): lax.all_gather(attended, 'fsdp', axis=0, tiled=True)  41.4 us
    all_to_all x1, waiting for transfers between devices, body(): lax.all_to_all(outgoing, 'seq', split_axis=1, concat_axis=1, tiled=True)  18.4 us
    unnamed x1, blocking collectives  13.9 us
    ppermute x7, starting transfers between devices, ring_gather(): later.append(lax.ppermute(later[-1], axis, down))  13.2 us
    unnamed x30, local copies, waits for them, and re-layouts  13.1 us
    ppermute x8, starting transfers between devices, ring_gather(): earlier.append(lax.ppermute(earlier[-1], axis, up))  11.7 us
  transfers between devices with their start and end apart: 17, of which 10 were waited for; matrix products, arithmetic and copies ran while one was open for 7% of the time, Pallas kernels for 0%

profile of v1, /device:TPU:1, one launch (start us, length us, event | category | flops | bytes accessed | tf_op | source)
XLA Modules:
  0.0 286.1 jit_solution(15214044055958823088)
XLA Ops:
  0.7 0.8 fusion.75
  1.5 0.6 reduce-window.6
  2.1 0.2 slice_reduce_fusion
  2.4 0.2 reduce-window.9
  2.8 1.3 dynamic-slice
  4.8 13.9 %all-reduce = s32[32]{0:T(128)S(1)} all-reduce(s32[32]{0:T(128)S(1)} %bitcast_dynamic-update-slice_fusion), channel_id=2, replica_groups=mesh['seq'=16,'fsdp'=16] {'seq'}, use_global_device_ids=true, to_apply=%add | all-reduce | flops 32 | bytes 256
  18.9 0.7 and_select_fusion
  19.6 3.5 %all-to-all-start.1 = ((s32[1,16,2]{2,0,1:T(1,128)}), s32[1,16,2]{2,0,1:T(1,128)S(1)}, u32[]{:S(2)}, u32[]{:S(2)}) async-start(s32[1,16,2]{2,0,1:T(1,128)} %and_select_fusion), calls=%async_computation.1 | async-start | bytes 16384 | tf_op jit(solution)/shard_map/all_to_all | solution.py:131
  23.2 5.4 %fusion.7 = bf16[2,16,2,32,1280]{4,3,1,0,2:T(8,128)(2,1)S(1)} fusion(s32[2,16,32]{2,1,0:T(8,128)S(1)} %broadcast_add_fusion, s32[2,512]{1,0:T(2,128)S(1)} %broadcast_add_fusion.1, pred[2,512]{1,0:T(4,128)(4,1)S(1)} %get-tuple-element.236, bf16[2,2,512,1280]{3,2,1,0:T(8,128)(2,1)} %param.14), kind=kOutput, calls=%fused_computation.15 | convolution fusion | flops 2688024576 | bytes 10494976 | tf_op jit(solution)/shard_map/rtsp,crpd->ctrsd/dot_general | solution.py:126
  28.6 2.8 copy.45
  31.5 6.8 %all-to-all-start = ((bf16[2,16,2,32,1280]{4,3,0,2,1:T(8,128)(2,1)}), bf16[2,16,2,32,1280]{4,3,0,2,1:T(8,128)(2,1)}, u32[]{:S(2)}, u32[]{:S(2)}) async-start(bf16[2,16,2,32,1280]{4,3,0,2,1:T(8,128)(2,1)} %copy.45), calls=%async_computation | async-start | bytes 10485760 | tf_op jit(solution)/shard_map/all_to_all | solution.py:130
  38.3 6.2 %collective-permute-start = (bf16[2,1280]{1,0:T(2,128)(2,1)S(1)}, bf16[2,1280]{1,0:T(2,128)(2,1)S(1)}, u32[]{:S(2)}, u32[]{:S(2)}) collective-permute-start(bf16[2,1280]{1,0:T(2,128)(2,1)S(1)} %copy-done.4), channel_id=1, source_target_pairs={{0,1},{1,2},{2,3},{3,4},{4,5},{5,6},{6,7},{7,8},{8,9},{9,10},{10,1... | collective-permute-start | bytes 15368 | tf_op jit(solution)/shard_map/ppermute | solution.py:18
  44.9 4.8 %fusion.5 = f32[2,32,1,2,1280]{4,2,3,1,0:T(1,128)S(1)} fusion(f32[2,32,16,1,1]{2,3,4,1,0:T(1,128)S(1)} %bitcast.192, bf16[2,2,32,16,1280]{4,3,2,1,0:T(8,128)(2,1)} %bitcast.189), kind=kOutput, calls=%fused_computation.13 | convolution fusion | flops 31457280 | bytes 5902336 | tf_op jit(solution)/shard_map/rbk,crbkd->crbd/dot_general | solution.py:105
  49.8 0.7 copy-done.2
  50.6 0.4 reshape_squeeze.13
  51.2 0.2 fusion.29
  51.5 0.2 fusion.74
  51.7 0.4 reshape_squeeze.15
  52.1 1.8 collective-permute-start.1
  53.9 0.2 fusion.27
  54.3 0.4 collective-permute-done.1
  54.6 2.3 collective-permute-start.2
  57.3 0.4 collective-permute-done.9
  57.7 0.6 collective-permute-start.10
  58.3 0.2 collective-permute-done.2
  58.5 1.4 collective-permute-start.3
  59.9 1.2 collective-permute-done.10
  61.1 1.8 collective-permute-start.11
  63.2 1.4 collective-permute-done.11
  64.6 3.1 %collective-permute-start.12 = (bf16[2,1280]{1,0:T(2,128)(2,1)S(1)}, bf16[2,1280]{1,0:T(2,128)(2,1)S(1)}, u32[]{:S(2)}, u32[]{:S(2)}) collective-permute-start(bf16[2,1280]{1,0:T(2,128)(2,1)S(1)} %collective-permute-done.11), channel_id=1, source_target_pairs={{0,15},{1,0},{2,1},{3,2},{4,3},{5,4},{6,5},{7,6},{8,7},{9,8},{10,9... | collective-permute-start | bytes 15368 | tf_op jit(solution)/shard_map/ppermute | solution.py:20
  67.7 0.7 collective-permute-done.12
  68.5 3.8 %collective-permute-start.13 = (bf16[2,1280]{1,0:T(2,128)(2,1)S(1)}, bf16[2,1280]{1,0:T(2,128)(2,1)S(1)}, u32[]{:S(2)}, u32[]{:S(2)}) collective-permute-start(bf16[2,1280]{1,0:T(2,128)(2,1)S(1)} %collective-permute-done.12), channel_id=1, source_target_pairs={{0,15},{1,0},{2,1},{3,2},{4,3},{5,4},{6,5},{7,6},{8,7},{9,8},{10,9... | collective-permute-start | bytes 15368 | tf_op jit(solution)/shard_map/ppermute | solution.py:20
  72.3 0.8 collective-permute-done.13
  73.1 3.8 %collective-permute-start.14 = (bf16[2,1280]{1,0:T(2,128)(2,1)S(1)}, bf16[2,1280]{1,0:T(2,128)(2,1)S(1)}, u32[]{:S(2)}, u32[]{:S(2)}) collective-permute-start(bf16[2,1280]{1,0:T(2,128)(2,1)S(1)} %collective-permute-done.13), channel_id=1, source_target_pairs={{0,15},{1,0},{2,1},{3,2},{4,3},{5,4},{6,5},{7,6},{8,7},{9,8},{10,9... | collective-permute-start | bytes 15368 | tf_op jit(solution)/shard_map/ppermute | solution.py:20
  77.0 0.7 collective-permute-done.14
  77.8 3.2 %collective-permute-done.7 = bf16[2,1280]{1,0:T(2,128)(2,1)S(1)} collective-permute-done((bf16[2,1280]{1,0:T(2,128)(2,1)S(1)}, bf16[2,1280]{1,0:T(2,128)(2,1)S(1)}, u32[]{:S(2)}, u32[]{:S(2)}) %collective-permute-start.7) | collective-permute-done | bytes 5152 | tf_op jit(solution)/shard_map/ppermute | solution.py:18
  80.9 5.2 %concatenate.6 = bf16[64,1280]{1,0:T(8,128)(2,1)} concatenate(bf16[2,1280]{1,0:T(2,128)(2,1)S(1)} %collective-permute-done.7, bf16[2,1280]{1,0:T(2,128)(2,1)S(1)} %collective-permute-done.6, bf16[2,1280]{1,0:T(2,128)(2,1)S(1)} %collective-permute-done.5, bf16[2,1280]{1,0:T(2,128)(2,1)S(1)} %collective-permute-done.4, bf16[2,1280]{1,0:T(2,128)(2,1)S(1)} %collective-permute-done.3, ...), dimensions={0} | concatenate | bytes 327680 | tf_op jit(solution)/shard_map/jit(_roll_dynamic)/concatenate | solution.py:22
  86.1 18.4 %all-to-all-done = bf16[2,16,2,32,1280]{4,3,0,2,1:T(8,128)(2,1)} async-done(((bf16[2,16,2,32,1280]{4,3,0,2,1:T(8,128)(2,1)}), bf16[2,16,2,32,1280]{4,3,0,2,1:T(8,128)(2,1)}, u32[]{:S(2)}, u32[]{:S(2)}) %all-to-all-start) | async-done | bytes 5242912 | tf_op jit(solution)/shard_map/all_to_all | solution.py:130
  104.5 5.7 %fusion.12 = bf16[2,2,1280,512,1]{3,2,1,0,4:T(8,128)(2,1)S(1)} fusion(bf16[2,16,2,32,1280]{4,3,0,2,1:T(8,128)(2,1)} %all-to-all-done, s32[2,16,32]{2,0,1:T(2,128)S(1)} %iota_add_fusion, pred[2,16,32]{2,0,1:T(4,128)(4,1)S(1)} %iota_compare_fusion.1), kind=kOutput, calls=%fused_computation.19 | convolution fusion | flops 2685403136 | bytes 10490880 | tf_op jit(solution)/shard_map/rlts,ctrsd->crld/dot_general | solution.py:146
  110.2 0.3 copy.109
  110.5 0.3 fusion.77
  110.9 1.9 copy-done.1
  112.8 0.4 fusion.80
  113.7 7.9 %copy.55 = bf16[2,2,512,1280]{3,2,1,0:T(8,128)(2,1)} copy(bf16[2,2,512,1280]{2,3,1,0:T(8,128)(2,1)} %bitcast.187) | data formatting | bytes 10485760
  121.6 0.8 fusion.47
  122.4 18.9 %all-gather.1 = f32[32,16,80]{2,1,0:T(8,128)S(1)} all-gather(f32[2,16,80]{2,1,0:T(8,128)S(1)} %multiply_add_fusion), channel_id=3, replica_groups=mesh['seq'=16,'fsdp'=16] {'seq'}, dimensions={0}, use_global_device_ids=true | all-gather | bytes 174080 | tf_op jit(solution)/shard_map/all_gather | solution.py:26
  141.4 16.3 %all_gather.34 = f32[16,2,16]{2,1,0:T(2,128)S(1)} all-gather(f32[1,2,16]{2,1,0:T(2,128)S(1)} %get-tuple-element.239), channel_id=1, replica_groups=mesh['seq'=16,'fsdp'=16] {'seq'}, dimensions={0}, use_global_device_ids=true | all-gather | bytes 2176 | tf_op jit(solution)/shard_map/all_gather | solution.py:26
  157.7 16.7 %all_gather.33 = f32[16,2,16]{2,1,0:T(2,128)S(1)} all-gather(f32[1,2,16]{2,1,0:T(2,128)S(1)} %get-tuple-element.240), channel_id=1, replica_groups=mesh['seq'=16,'fsdp'=16] {'seq'}, dimensions={0}, use_global_device_ids=true | all-gather | bytes 2176 | tf_op jit(solution)/shard_map/all_gather | solution.py:26
  174.4 1.5 while.19
  176.1 41.4 %all-gather.2 = bf16[16,2,1280]{2,1,0:T(2,128)(2,1)S(1)} all-gather(bf16[1,2,1280]{2,1,0:T(2,128)(2,1)S(1)} %reshape.373), channel_id=1, replica_groups=mesh['seq'=16,'fsdp'=16] {'fsdp'}, dimensions={0}, use_global_device_ids=true | all-gather | bytes 87040 | tf_op jit(solution)/shard_map/all_gather | solution.py:180
  217.5 0.9 fusion.59
  218.4 14.8 %all-gather.3 = bf16[16,80,32]{1,2,0:T(8,128)(2,1)S(1)} all-gather(bf16[1,80,32]{1,2,0:T(8,128)(2,1)S(1)} %fusion.59), channel_id=1, replica_groups=mesh['seq'=16,'fsdp'=16] {'fsdp'}, dimensions={0}, use_global_device_ids=true | all-gather | bytes 87040 | tf_op jit(solution)/shard_map/all_gather | solution.py:174
  233.3 0.2 reshape.376
  233.6 1.2 fusion.55
  234.8 16.1 %all-gather.4 = bf16[16,80,32]{1,2,0:T(8,128)(2,1)S(1)} all-gather(bf16[1,80,32]{1,2,0:T(8,128)(2,1)S(1)} %fusion.55), channel_id=1, replica_groups=mesh['seq'=16,'fsdp'=16] {'fsdp'}, dimensions={0}, use_global_device_ids=true | all-gather | bytes 87040 | tf_op jit(solution)/shard_map/all_gather | solution.py:174
  251.0 0.2 reshape.378
  251.2 1.1 fusion.19
  252.3 14.8 %all-gather.5 = bf16[16,80,32]{1,2,0:T(8,128)(2,1)S(1)} all-gather(bf16[1,80,32]{1,2,0:T(8,128)(2,1)S(1)} %fusion.19), channel_id=1, replica_groups=mesh['seq'=16,'fsdp'=16] {'fsdp'}, dimensions={0}, use_global_device_ids=true | all-gather | bytes 87040 | tf_op jit(solution)/shard_map/all_gather | solution.py:174
  267.2 0.2 reshape.380
  267.5 0.3 fusion.17
  267.8 16.5 %all-gather.6 = bf16[16,240,32]{1,2,0:T(8,128)(2,1)S(1)} all-gather(bf16[1,240,32]{1,2,0:T(8,128)(2,1)S(1)} %fusion.17), channel_id=1, replica_groups=mesh['seq'=16,'fsdp'=16] {'fsdp'}, dimensions={0}, use_global_device_ids=true | all-gather | bytes 261120 | tf_op jit(solution)/shard_map/all_gather | solution.py:174
  284.5 0.4 reshape.382
  284.9 0.6 dynamic-slice_bitcast_fusion.1
  285.5 0.6 dynamic-slice_bitcast_fusion
  (121 shorter events, 5.2 us)
Async XLA Ops:
  0.6 266.9 %copy-start = (bf16[1280,240]{0,1:T(8,128)(2,1)S(1)}, bf16[1280,240]{0,1:T(8,128)(2,1)}, u32[]{:S(2)}) copy-start(bf16[1280,240]{0,1:T(8,128)(2,1)} %param.23) | copy-start | bytes 1843204
  19.6 11.9 %all-to-all-start.1 = ((s32[1,16,2]{2,0,1:T(1,128)}), s32[1,16,2]{2,0,1:T(1,128)S(1)}, u32[]{:S(2)}, u32[]{:S(2)}) async-start(s32[1,16,2]{2,0,1:T(1,128)} %and_select_fusion), calls=%async_computation.1 | async-start | bytes 16384 | tf_op jit(solution)/shard_map/all_to_all | solution.py:131
  31.5 6.8 %copy-start.4 = (bf16[2,1280]{1,0:T(2,128)(2,1)S(1)}, bf16[2,1280]{1,0:T(2,128)(2,1)}, u32[]{:S(2)}) copy-start(bf16[2,1280]{1,0:T(2,128)(2,1)} %param.19) | copy-start | bytes 15364
  31.5 13.1 %copy-start.7 = (f32[2,512]{1,0:T(2,128)S(1)}, f32[2,512]{1,0:T(2,128)}, u32[]{:S(2)}) copy-start(f32[2,512]{1,0:T(2,128)} %param.16) | copy-start | bytes 12292
  31.5 13.2 %copy-start.5 = (bf16[2,3840]{1,0:T(2,128)(2,1)S(1)}, bf16[2,3840]{1,0:T(2,128)(2,1)}, u32[]{:S(2)}) copy-start(bf16[2,3840]{1,0:T(2,128)(2,1)} %param.18) | copy-start | bytes 46084
  31.5 73.0 %all-to-all-start = ((bf16[2,16,2,32,1280]{4,3,0,2,1:T(8,128)(2,1)}), bf16[2,16,2,32,1280]{4,3,0,2,1:T(8,128)(2,1)}, u32[]{:S(2)}, u32[]{:S(2)}) async-start(bf16[2,16,2,32,1280]{4,3,0,2,1:T(8,128)(2,1)} %copy.45), calls=%async_computation | async-start | bytes 10485760 | tf_op jit(solution)/shard_map/all_to_all | solution.py:130
  38.3 13.8 %collective-permute-start = (bf16[2,1280]{1,0:T(2,128)(2,1)S(1)}, bf16[2,1280]{1,0:T(2,128)(2,1)S(1)}, u32[]{:S(2)}, u32[]{:S(2)}) collective-permute-start(bf16[2,1280]{1,0:T(2,128)(2,1)S(1)} %copy-done.4), channel_id=1, source_target_pairs={{0,1},{1,2},{2,3},{3,4},{4,5},{5,6},{6,7},{7,8},{8,9},{9,10},{10,1... | collective-permute-start | bytes 15368 | tf_op jit(solution)/shard_map/ppermute | solution.py:18
  44.5 9.7 %collective-permute-start.8 = (bf16[2,1280]{1,0:T(2,128)(2,1)S(1)}, bf16[2,1280]{1,0:T(2,128)(2,1)S(1)}, u32[]{:S(2)}, u32[]{:S(2)}) collective-permute-start(bf16[2,1280]{1,0:T(2,128)(2,1)S(1)} %copy-done.4), channel_id=1, source_target_pairs={{0,15},{1,0},{2,1},{3,2},{4,3},{5,4},{6,5},{7,6},{8,7},{9,8},{10,9... | collective-permute-start | bytes 15368 | tf_op jit(solution)/shard_map/ppermute | solution.py:20
  49.8 0.7 copy-start.2
  52.1 2.5 collective-permute-start.1
  54.2 3.5 %collective-permute-start.9 = (bf16[2,1280]{1,0:T(2,128)(2,1)S(1)}, bf16[2,1280]{1,0:T(2,128)(2,1)S(1)}, u32[]{:S(2)}, u32[]{:S(2)}) collective-permute-start(bf16[2,1280]{1,0:T(2,128)(2,1)S(1)} %collective-permute-done.8), channel_id=1, source_target_pairs={{0,15},{1,0},{2,1},{3,2},{4,3},{5,4},{6,5},{7,6},{8,7},{9,8},{10,9... | collective-permute-start | bytes 15368 | tf_op jit(solution)/shard_map/ppermute | solution.py:20
  54.6 3.9 %collective-permute-start.2 = (bf16[2,1280]{1,0:T(2,128)(2,1)S(1)}, bf16[2,1280]{1,0:T(2,128)(2,1)S(1)}, u32[]{:S(2)}, u32[]{:S(2)}) collective-permute-start(bf16[2,1280]{1,0:T(2,128)(2,1)S(1)} %collective-permute-done.1), channel_id=1, source_target_pairs={{0,1},{1,2},{2,3},{3,4},{4,5},{5,6},{6,7},{7,8},{8,9},{9,10},{10,1... | collective-permute-start | bytes 15368 | tf_op jit(solution)/shard_map/ppermute | solution.py:18
  57.7 3.4 %collective-permute-start.10 = (bf16[2,1280]{1,0:T(2,128)(2,1)S(1)}, bf16[2,1280]{1,0:T(2,128)(2,1)S(1)}, u32[]{:S(2)}, u32[]{:S(2)}) collective-permute-start(bf16[2,1280]{1,0:T(2,128)(2,1)S(1)} %collective-permute-done.9), channel_id=1, source_target_pairs={{0,15},{1,0},{2,1},{3,2},{4,3},{5,4},{6,5},{7,6},{8,7},{9,8},{10,9... | collective-permute-start | bytes 15368 | tf_op jit(solution)/shard_map/ppermute | solution.py:20
  58.5 4.4 %collective-permute-start.3 = (bf16[2,1280]{1,0:T(2,128)(2,1)S(1)}, bf16[2,1280]{1,0:T(2,128)(2,1)S(1)}, u32[]{:S(2)}, u32[]{:S(2)}) collective-permute-start(bf16[2,1280]{1,0:T(2,128)(2,1)S(1)} %collective-permute-done.2), channel_id=1, source_target_pairs={{0,1},{1,2},{2,3},{3,4},{4,5},{5,6},{6,7},{7,8},{8,9},{9,10},{10,1... | collective-permute-start | bytes 15368 | tf_op jit(solution)/shard_map/ppermute | solution.py:18
  61.1 3.4 %collective-permute-start.11 = (bf16[2,1280]{1,0:T(2,128)(2,1)S(1)}, bf16[2,1280]{1,0:T(2,128)(2,1)S(1)}, u32[]{:S(2)}, u32[]{:S(2)}) collective-permute-start(bf16[2,1280]{1,0:T(2,128)(2,1)S(1)} %collective-permute-done.10), channel_id=1, source_target_pairs={{0,15},{1,0},{2,1},{3,2},{4,3},{5,4},{6,5},{7,6},{8,7},{9,8},{10,9... | collective-permute-start | bytes 15368 | tf_op jit(solution)/shard_map/ppermute | solution.py:20
  63.0 4.7 %collective-permute-start.4 = (bf16[2,1280]{1,0:T(2,128)(2,1)S(1)}, bf16[2,1280]{1,0:T(2,128)(2,1)S(1)}, u32[]{:S(2)}, u32[]{:S(2)}) collective-permute-start(bf16[2,1280]{1,0:T(2,128)(2,1)S(1)} %collective-permute-done.3), channel_id=1, source_target_pairs={{0,1},{1,2},{2,3},{3,4},{4,5},{5,6},{6,7},{7,8},{8,9},{9,10},{10,1... | collective-permute-start | bytes 15368 | tf_op jit(solution)/shard_map/ppermute | solution.py:18
  64.6 3.9 %collective-permute-start.12 = (bf16[2,1280]{1,0:T(2,128)(2,1)S(1)}, bf16[2,1280]{1,0:T(2,128)(2,1)S(1)}, u32[]{:S(2)}, u32[]{:S(2)}) collective-permute-start(bf16[2,1280]{1,0:T(2,128)(2,1)S(1)} %collective-permute-done.11), channel_id=1, source_target_pairs={{0,15},{1,0},{2,1},{3,2},{4,3},{5,4},{6,5},{7,6},{8,7},{9,8},{10,9... | collective-permute-start | bytes 15368 | tf_op jit(solution)/shard_map/ppermute | solution.py:20
  67.6 4.7 %collective-permute-start.5 = (bf16[2,1280]{1,0:T(2,128)(2,1)S(1)}, bf16[2,1280]{1,0:T(2,128)(2,1)S(1)}, u32[]{:S(2)}, u32[]{:S(2)}) collective-permute-start(bf16[2,1280]{1,0:T(2,128)(2,1)S(1)} %collective-permute-done.4), channel_id=1, source_target_pairs={{0,1},{1,2},{2,3},{3,4},{4,5},{5,6},{6,7},{7,8},{8,9},{9,10},{10,1... | collective-permute-start | bytes 15368 | tf_op jit(solution)/shard_map/ppermute | solution.py:18
  68.5 4.7 %collective-permute-start.13 = (bf16[2,1280]{1,0:T(2,128)(2,1)S(1)}, bf16[2,1280]{1,0:T(2,128)(2,1)S(1)}, u32[]{:S(2)}, u32[]{:S(2)}) collective-permute-start(bf16[2,1280]{1,0:T(2,128)(2,1)S(1)} %collective-permute-done.12), channel_id=1, source_target_pairs={{0,15},{1,0},{2,1},{3,2},{4,3},{5,4},{6,5},{7,6},{8,7},{9,8},{10,9... | collective-permute-start | bytes 15368 | tf_op jit(solution)/shard_map/ppermute | solution.py:20
  72.3 4.7 %collective-permute-start.6 = (bf16[2,1280]{1,0:T(2,128)(2,1)S(1)}, bf16[2,1280]{1,0:T(2,128)(2,1)S(1)}, u32[]{:S(2)}, u32[]{:S(2)}) collective-permute-start(bf16[2,1280]{1,0:T(2,128)(2,1)S(1)} %collective-permute-done.5), channel_id=1, source_target_pairs={{0,1},{1,2},{2,3},{3,4},{4,5},{5,6},{6,7},{7,8},{8,9},{9,10},{10,1... | collective-permute-start | bytes 15368 | tf_op jit(solution)/shard_map/ppermute | solution.py:18
  73.1 4.7 %collective-permute-start.14 = (bf16[2,1280]{1,0:T(2,128)(2,1)S(1)}, bf16[2,1280]{1,0:T(2,128)(2,1)S(1)}, u32[]{:S(2)}, u32[]{:S(2)}) collective-permute-start(bf16[2,1280]{1,0:T(2,128)(2,1)S(1)} %collective-permute-done.13), channel_id=1, source_target_pairs={{0,15},{1,0},{2,1},{3,2},{4,3},{5,4},{6,5},{7,6},{8,7},{9,8},{10,9... | collective-permute-start | bytes 15368 | tf_op jit(solution)/shard_map/ppermute | solution.py:20
  77.0 4.0 %collective-permute-start.7 = (bf16[2,1280]{1,0:T(2,128)(2,1)S(1)}, bf16[2,1280]{1,0:T(2,128)(2,1)S(1)}, u32[]{:S(2)}, u32[]{:S(2)}) collective-permute-start(bf16[2,1280]{1,0:T(2,128)(2,1)S(1)} %collective-permute-done.6), channel_id=1, source_target_pairs={{0,1},{1,2},{2,3},{3,4},{4,5},{5,6},{6,7},{7,8},{8,9},{9,10},{10,1... | collective-permute-start | bytes 15368 | tf_op jit(solution)/shard_map/ppermute | solution.py:18
  110.5 2.3 copy-start.1
  113.7 103.8 %copy-start.3 = (bf16[1280,80]{0,1:T(8,128)(2,1)S(1)}, bf16[1280,80]{0,1:T(8,128)(2,1)}, u32[]{:S(2)}) copy-start(bf16[1280,80]{0,1:T(8,128)(2,1)} %param.20) | copy-start | bytes 614404
  113.7 119.9 %copy-start.8 = (f32[1280]{0:T(1024)S(1)}, f32[1280]{0:T(1024)}, u32[]{:S(2)}) copy-start(f32[1280]{0:T(1024)} %param.24) | copy-start | bytes 15364
  121.6 145.9 %copy-start.6 = (f32[1280]{0:T(1024)S(1)}, f32[1280]{0:T(1024)}, u32[]{:S(2)}) copy-start(f32[1280]{0:T(1024)} %param.25) | copy-start | bytes 15364
